TPU v7x, 128 devices: a whole 4x4x4 slice. The times are simulated.
128 devices in a mesh: island: 4 (over x), expert: 16 (over z, y), tensor: 2 (over core).
Axes of the slice: x: 4, y: 4, z: 4, core: 2. Of those that a mesh axis runs over, the one named last changes fastest.
Arguments:
- tokens: bfloat16 [4, 4096, 2048], P('island', 'expert', 'tensor'), may hold values from -6 to 6
- token_grads: bfloat16 [4, 4096, 2048], P('island', 'expert', 'tensor'), may hold values from -6 to 6
- slot_token: int32 [4, 16, 16, 96], P('island', 'expert'), may hold values from 0 to 255, as said below
- slot_count: int32 [4, 16, 16], P('island', 'expert'), may hold values from 24 to 96, as said below
- slot_prob: float32 [4, 16, 16, 96], P('island', 'expert'), may hold values from 0.1 to 1
- gate_weight: bfloat16 [4, 16, 2048, 1536], P('island', 'expert', None, 'tensor'), may hold values from -0.125 to 0.125
- down_weight: bfloat16 [4, 16, 1536, 2048], P('island', 'expert', 'tensor'), may hold values from -0.15625 to 0.15625
- drift: bfloat16 [4, 16, 2048, 1536], P('island', 'expert', None, 'tensor'), may hold values from -6 to 6
- momentum: float32 [16, 2048, 1536], P('expert', None, 'tensor'), may hold values from -1.5 to 1.5
Outputs:
- new_momentum: float32 [16, 2048, 1536], P('expert', None, 'tensor')
- outer_step: bfloat16 [16, 2048, 1536], P('expert', None, 'tensor')
Inputs may be any that keep to these rules, and one draw needn't show every extreme that they name: `slot_token`: for each island, source device and expert the 96 entries are distinct tokens of that source device. `slot_count`: in every island some expert is full from every source device.
All inputs are finite; a program needn't handle non-finite values.
Results may differ from a plain program's by a relative error of at most 0.0031.
The roundings to bfloat16 on the way count: a program that leaves them out, or rounds other values in their place, can miss the bound.
Values may be sent and summed in bfloat16 or wider, within the bound.
A program may use at most 128 MiB of HBM per device.

v0:
```python
import math

import jax
import jax.numpy as jnp
from jax import lax
from jax.sharding import PartitionSpec as P


def side_by_side(arrays, axis, split_dim, concat_dim, along):
    widths = [a.shape[along] for a in arrays]
    both = jnp.concatenate(arrays, axis=along)
    whole = lax.all_to_all(both, axis, split_axis=split_dim, concat_axis=concat_dim, tiled=True)
    return tuple(jnp.split(whole, [sum(widths[:k]) for k in range(1, len(widths))], axis=along))


def in_one_piece(arrays, axis, dim, along):
    both = jnp.concatenate(arrays, axis=along)
    whole, at, done = (lax.all_gather(both, axis, axis=dim, tiled=True), 0, [])
    for a in arrays:
        done.append(lax.slice_in_dim(whole, at, at + a.shape[along], axis=along))
        at += a.shape[along]
    return tuple(done)


def copy_for_each(array, axis):
    size = lax.axis_size(axis)
    return lax.all_to_all(
        jnp.broadcast_to(array[None], (size, *array.shape)), axis, 0, 0, tiled=True
    )


def taken_together(array, axis):
    return copy_for_each(array, axis).sum(axis=0)


def outer_update(average, old_moment, square_sum, entries):
    clip_scale = jnp.minimum(1.0, 0.25 * math.sqrt(entries) / jnp.sqrt(square_sum + 1e-06))
    clipped = clip_scale * average
    new_moment = 0.9 * old_moment + clipped
    step_value = (0.7 * (clipped + 0.9 * new_moment)).astype(jnp.bfloat16)
    return (new_moment, step_value)


def body(
    tokens,
    token_grads,
    slot_token,
    slot_count,
    slot_prob,
    gate_weight,
    down_weight,
    drift,
    momentum,
):
    index_table = slot_token[0, 0]
    filled = slot_count[0, 0]
    live_slots = lax.broadcasted_iota(jnp.int32, index_table.shape, 1) < filled[:, None]
    slot_weights = jnp.where(live_slots, slot_prob[0, 0], jnp.float32(0.0))[..., None]
    input_slots = jnp.where(
        live_slots[..., None], tokens[0][index_table], jnp.zeros((), jnp.bfloat16)
    )
    grad_slots = (slot_weights * token_grads[0][index_table].astype(jnp.float32)).astype(
        jnp.bfloat16
    )
    input_slots, grad_slots = (input_slots, grad_slots)
    part_inputs, part_grads = side_by_side((input_slots, grad_slots), "expert", 0, 1, 2)
    inputs, out_grads = in_one_piece((part_inputs, part_grads), "tensor", 2, 0)
    gate_value = jnp.einsum(
        "erd,edf->erf", inputs, gate_weight[0], preferred_element_type=jnp.float32
    )
    back_grad = jnp.einsum(
        "erd,efd->erf", out_grads, down_weight[0], preferred_element_type=jnp.float32
    )
    hidden_grad = (back_grad * jax.nn.silu(gate_value)).astype(jnp.bfloat16)
    gradient = jnp.einsum("erd,erf->edf", inputs, hidden_grad, preferred_element_type=jnp.float32)
    entries = gradient.size * lax.axis_size("expert") * lax.axis_size("tensor")
    inner_square = taken_together(jnp.sum(gradient * gradient), ("expert", "tensor"))
    inner_scale = jnp.minimum(1.0, math.sqrt(entries) / jnp.sqrt(inner_square + 1e-06))
    pseudo = drift[0].astype(jnp.float32) + inner_scale * gradient
    islands = lax.axis_size("island")
    average = lax.psum(pseudo, "island") / islands
    outer_square = taken_together(jnp.sum(average * average), ("expert", "tensor"))
    new_momentum, outer_step = outer_update(average, momentum, outer_square, entries)
    return (new_momentum, outer_step)


def solution(mesh):
    return jax.shard_map(
        body,
        mesh=mesh,
        in_specs=(
            P("island", "expert", "tensor"),
            P("island", "expert", "tensor"),
            P("island", "expert", None, None),
            P("island", "expert", None),
            P("island", "expert", None, None),
            P("island", "expert", None, "tensor"),
            P("island", "expert", "tensor", None),
            P("island", "expert", None, "tensor"),
            P("expert", None, "tensor"),
        ),
        out_specs=(P("expert", None, "tensor"), P("expert", None, "tensor")),
        check_vma=False,
    )
```

profile of v0, /device:TPU:1, one launch (start us, length us, event | category | flops | bytes accessed | tf_op | source)
XLA Modules:
  0.0 363.5 jit_solution(14872693927592940044)
XLA Ops:
  7.2 0.0 copy-start
  7.2 0.0 all-gather.2.cloned.1.call-start
  7.2 0.9 iota_compare_fusion
  8.1 0.7 compare_select_fusion
  8.8 0.1 reshape.129
  8.9 0.8 bitcast_select_fusion
  9.7 8.9 %gather_fusion.1 = bf16[1536,1024]{1,0:T(8,128)(2,1)} fusion(bf16[256,1024]{1,0:T(8,128)(2,1)} %bitcast.43, s32[2048]{0:T(1024)S(1)} %pad_clamp_fusion), kind=kCustom, calls=%fused_computation.1 | custom fusion | bytes 6297600 | tf_op jit(solution)/shard_map/gather | solution.py:62
  18.6 8.9 %gather_fusion = bf16[1536,1024]{1,0:T(8,128)(2,1)} fusion(bf16[256,1024]{1,0:T(8,128)(2,1)} %bitcast.44, s32[2048]{0:T(1024)S(1)} %pad_clamp_fusion), kind=kCustom, calls=%fused_computation | custom fusion | bytes 6297600 | tf_op jit(solution)/shard_map/gather | solution.py:60
  27.5 0.0 copy-start.1
  27.5 2.6 fusion.1
  30.1 0.2 copy-done.1
  30.3 1.8 broadcast_select_fusion
  32.1 2.7 pad_maximum_fusion
  34.9 80.6 %all_to_all.24 = bf16[16,96,2048]{2,1,0:T(8,128)(2,1)S(1)} all-to-all(bf16[16,96,2048]{2,1,0:T(8,128)(2,1)S(1)} %pad_maximum_fusion), channel_id=1, replica_groups=mesh['island'=4,'expert'=16,'tensor'=2] {'expert'}, dimensions={0} | all-to-all | bytes 12582912 | tf_op jit(solution)/shard_map/all_to_all | solution.py:12
  115.5 0.7 fusion.11
  116.2 3.2 pad_maximum_fusion.1
  119.4 0.0 all-gather.2.cloned.1.call-update
  119.5 0.0 all-reduce.2.cloned.1.call-start
  119.5 26.8 %all-gather.2.cloned.1.call-done = bf16[2,1536,2048]{2,1,0:T(8,128)(2,1)} async-done(((bf16[2,1536,1024]{2,1,0:T(8,128)(2,1)}), bf16[2,1536,2048]{2,1,0:T(8,128)(2,1)}) %all-gather.2.cloned.1.call-update) | async-done | bytes 12582928 | tf_op jit(solution)/shard_map/all_gather | solution.py:18
  146.3 9.5 %fusion.4 = f32[1536,768]{1,0:T(8,128)} fusion(bf16[2,1536,2048]{2,1,0:T(8,128)(2,1)} %all-gather.2.cloned.1.call-done, bf16[1,1,2048,768]{3,2,1,0:T(8,128)(2,1)} %param.14), kind=kOutput, calls=%fused_computation.16 | convolution fusion | flops 4831838208 | bytes 14155776 | tf_op jit(solution)/shard_map/erd,edf->erf/dot_general | solution.py:68
  155.8 0.0 copy-done
  155.8 21.8 %multiply_reduce_fusion.1 = (f32[]{:T(128)}, f32[2048,768]{1,0:T(8,128)}) fusion(f32[1536,768]{1,0:T(8,128)} %fusion.4, bf16[2,1536,2048]{2,1,0:T(8,128)(2,1)} %all-gather.2.cloned.1.call-done, bf16[1,1,768,2048]{3,2,1,0:T(8,128)(2,1)S(1)} %copy-done), kind=kOutput, calls=%fused_computation.13 | convolution fusion | flops 9673900032 | bytes 26738692 | tf_op jit(solution)/shard_map/erd,erf->edf/dot_general | solution.py:75
  177.6 0.7 broadcast_in_dim.35
  178.3 14.1 %all_to_all.25 = f32[32,1,1]{2,1,0:T(1,128)S(1)} all-to-all(f32[32,1,1]{2,1,0:T(1,128)S(1)} %broadcast_in_dim.35), channel_id=1, replica_groups=mesh['island'=4,'expert'=16,'tensor'=2] {'expert','tensor'}, dimensions={0} | all-to-all | bytes 256 | tf_op jit(solution)/shard_map/all_to_all | solution.py:27
  192.4 0.6 reduce_sum.37
  193.7 7.3 %fusion.2 = f32[1,2048,768]{2,1,0:T(8,128)} fusion(f32[2048,768]{1,0:T(8,128)} %get-tuple-element.7, bf16[1,1,2048,768]{3,2,1,0:T(8,128)(2,1)} %param.16, f32[]{:T(128)S(6)} %min.6), kind=kLoop, calls=%fused_computation.10 | loop fusion | flops 4718592 | bytes 15728644 | tf_op jit(solution)/shard_map/add | solution.py:79
  201.0 0.0 all-reduce.2.cloned.1.call-update
  201.0 124.3 %all-reduce.2.cloned.1.call-done = f32[1,2048,768]{2,1,0:T(8,128)} async-done(((f32[1,2048,768]{2,1,0:T(8,128)}), f32[1,2048,768]{2,1,0:T(8,128)}) %all-reduce.2.cloned.1.call-update) | async-done | bytes 6291472 | tf_op jit(solution)/shard_map/psum | solution.py:81
  325.3 5.0 %multiply_reduce_fusion = f32[]{:T(128)} fusion(f32[1,2048,768]{2,1,0:T(8,128)} %all-reduce.2.cloned.1.call-done), kind=kLoop, calls=%fused_computation.12 | loop fusion | flops 4718591 | bytes 6291460 | tf_op jit(solution)/shard_map/reduce_sum | solution.py:82
  330.3 0.7 broadcast_in_dim.36
  330.9 14.6 %all_to_all.26 = f32[32,1,1]{2,1,0:T(1,128)S(1)} all-to-all(f32[32,1,1]{2,1,0:T(1,128)S(1)} %broadcast_in_dim.36), channel_id=1, replica_groups=mesh['island'=4,'expert'=16,'tensor'=2] {'expert','tensor'}, dimensions={0} | all-to-all | bytes 256 | tf_op jit(solution)/shard_map/all_to_all | solution.py:27
  345.6 0.6 reduce_sum.39
  346.9 9.8 %multiply_convert_fusion = (bf16[1,2048,768]{2,1,0:T(8,128)(2,1)}, f32[1,2048,768]{2,1,0:T(8,128)}) fusion(f32[1,2048,768]{2,1,0:T(8,128)} %all-reduce.2.cloned.1.call-done, f32[]{:T(128)S(6)} %mul.60, f32[1,2048,768]{2,1,0:T(8,128)} %param.17), kind=kLoop, calls=%fused_computation.11 | loop fusion | flops 11010048 | bytes 22020100 | tf_op jit(solution)/shard_map/convert_element_type | solution.py:40
  (1 shorter events, 0.0 us)
Async XLA Ops:
  7.2 148.6 %copy-start = (bf16[1,1,768,2048]{3,2,1,0:T(8,128)(2,1)S(1)}, bf16[1,1,768,2048]{3,2,1,0:T(8,128)(2,1)}, u32[]{:S(2)}) copy-start(bf16[1,1,768,2048]{3,2,1,0:T(8,128)(2,1)} %param.15) | copy-start | bytes 9437188
  7.2 139.1 %all-gather.2.cloned.1.call-start = ((), (), s32[]{:S(2)}) async-start(), calls=%async_computation.3 | async-start | bytes 18874368 | tf_op jit(solution)/shard_map/all_gather | solution.py:18
  27.5 2.8 copy-start.1
  119.5 205.8 %all-reduce.2.cloned.1.call-start = ((), (), s32[]{:S(2)}) async-start(), calls=%async_computation.4 | async-start | bytes 12582912 | tf_op jit(solution)/shard_map/psum | solution.py:81
Sparse Core Ops, SparseCore 0:
  119.6 26.6 all-gather.1
  201.1 124.1 all-reduce.1
where the time goes:
time: 364 us
  waiting for transfers between devices  151 us (41%)
  blocking collectives  109 us (30%)
  other arithmetic  36.1 us (10%)
  matrix products  31.3 us (9%)
  local copies, waits for them, and re-layouts  20.1 us (6%)
  between operations  15.5 us (4%)
    psum x1, waiting for transfers between devices, body(): average = lax.psum(pseudo, 'island') / islands  124 us
    all_to_all x1, blocking collectives, side_by_side(): lax.all_to_all(both, axis, split_axis=split_dim, concat_axis=concat_dim,...  80.6 us
    all_to_all x2, blocking collectives, copy_for_each(): lax.all_to_all(jnp.broadcast_to(array[None], (size, *array.shape)), axis,...  28.8 us
    all_gather x1, waiting for transfers between devices, in_one_piece(): whole, at, done = (lax.all_gather(both, axis, axis=dim, tiled=True), 0, [])  26.8 us
    dot_general x1, matrix products, body(): jnp.einsum('erd,erf->edf', inputs, hidden_grad, preferred_element_type=jn...  21.8 us
    convert_element_type x1, other arithmetic, outer_update(): step_value = (0.7 * (clipped + 0.9 * new_moment)).astype(jnp.bfloat16)  9.79 us
    dot_general x1, matrix products, body(): jnp.einsum('erd,edf->erf', inputs, gate_weight[0], preferred_element_type...  9.45 us
    gather x1, local copies, waits for them, and re-layouts, body(): token_grads[0][index_table].astype(jnp.float32)  8.88 us
  transfers between devices with their start and end apart: 2, of which 2 were waited for; matrix products, arithmetic and copies ran while one was open for 0% of the time, Pallas kernels for 0%

commit v1 on v0

v1 whole, which is shorter than its diff:
```python
import functools
import math

import jax
import jax.numpy as jnp
from jax import lax
from jax.experimental import pallas as pl
from jax.experimental.pallas import tpu as pltpu
from jax.sharding import PartitionSpec as P

MESH = pl.DeviceIdType.MESH
BF16 = jnp.bfloat16
F32 = jnp.float32
AVG = jnp.bfloat16
N = 4
CAP = 96
GROUP = N * CAP
ROWS = N * GROUP
TOK = 256
HALF = 1024
FEAT = 2 * HALF
QUART = FEAT // N
HID = 768
TILE = 256
ENTRIES = 16 * 2048 * 1536


def back(k):
    return (N - k) % N


def kernel(
    tok_ref, tg_ref, tab_ref, wg_ref, wd_ref, drift_ref,
    avg_ref, sq_ref,
    tok_z, tg_y, tab_z, tab_y, send_x, send_g, relay_x, relay_g, xs, gs, wg, wd,
    gate, backg, xt, hid, g_own, g_send, g_relay, g_recv, d_recv, avg_all,
    part, tiles, send_sem, recv_sem, local_sem,
):
    x = lax.axis_index("island")
    ex = lax.axis_index("expert")
    t = lax.axis_index("tensor")
    z, y = ex // N, lax.rem(ex, N)

    def at_x(k):
        return {"island": lax.rem(x + k, N)}

    def at_z(k):
        return {"expert": lax.rem(z + k, N) * N + y}

    def at_y(k):
        return {"expert": z * N + lax.rem(y + k, N)}

    partner = {"tensor": 1 - t}
    started = []
    local_count = [0]

    def push(src, dst, device):
        i = len(started)
        copy = pltpu.make_async_remote_copy(
            src_ref=src, dst_ref=dst, send_sem=send_sem.at[i], recv_sem=recv_sem.at[i],
            device_id=device, device_id_type=MESH,
        )
        copy.start()
        started.append(copy)
        return copy

    def fetch(src, dst):
        copy = pltpu.make_async_copy(src, dst, local_sem.at[local_count[0]])
        local_count[0] += 1
        copy.start()
        return copy

    own_tok = fetch(tok_ref, tok_z.at[0])
    own_tab = fetch(tab_ref, tab_z.at[0])
    own_tab2 = fetch(tab_ref, tab_y.at[0])
    own_tg = fetch(tg_ref, tg_y.at[0])
    own_half = pl.ds(pl.multiple_of(t * HALF, HALF), HALF)
    other_half = pl.ds(pl.multiple_of((1 - t) * HALF, HALF), HALF)
    loads = [
        fetch(wg_ref.at[own_half, :], wg.at[0]),
        fetch(wg_ref.at[other_half, :], wg.at[1]),
        fetch(wd_ref.at[:, own_half], wd.at[0]),
        fetch(wd_ref.at[:, other_half], wd.at[1]),
    ]

    def quarter(k):
        return pl.ds(pl.multiple_of(lax.rem(x + k, N) * QUART, QUART), QUART)

    own_drift = fetch(drift_ref.at[quarter(0), :], d_recv.at[0])

    barrier = pltpu.get_barrier_semaphore()
    peers = [at(k) for at in (at_x, at_y, at_z) for k in (1, 2, 3)] + [partner]
    for peer in peers:
        pl.semaphore_signal(barrier, inc=1, device_id=peer, device_id_type=MESH)
    pl.semaphore_wait(barrier, len(peers))

    tz = {k: push(tab_ref, tab_z.at[back(k)], at_z(k)) for k in (1, 3, 2)}
    ty = {k: push(tab_ref, tab_y.at[back(k)], at_y(k)) for k in (1, 3, 2)}
    tok_up = push(tok_ref, tok_z.at[3], at_z(1))
    tok_down = push(tok_ref, tok_z.at[1], at_z(3))
    tg_up = push(tg_ref, tg_y.at[3], at_y(1))
    tg_down = push(tg_ref, tg_y.at[1], at_y(3))
    drifts = [push(drift_ref.at[quarter(k), :], d_recv.at[back(k)], at_x(k)) for k in (2, 1, 3)]

    lane = lax.broadcasted_iota(jnp.int32, (CAP, 128), 1)
    token_of = lax.broadcasted_iota(jnp.int32, (CAP, TOK), 1).astype(F32)

    def column(tab, at):
        return jnp.sum(jnp.where(lane == at, tab, 0.0), axis=1, keepdims=True)

    def picked(tab, rows, expert, weighted):
        chosen = jnp.where(column(tab, expert) == token_of, 1.0, 0.0).astype(BF16)
        out = jnp.dot(chosen, rows, preferred_element_type=F32)
        if weighted:
            out = out * column(tab, expert + 16)
        return out.astype(BF16)

    chunk = {}
    relays = {}

    def scatter_x(kz):
        tab, rows = tab_z[kz], tok_z[kz]
        for ky in (2, 1, 3, 0):
            expert = z * N + lax.rem(y + ky, N)
            got = picked(tab, rows, expert, False)
            if ky == 0:
                xs[0, kz, 0] = got
                continue
            send_x[ky - 1, kz] = got
            src = send_x.at[ky - 1, kz]
            if ky == 2:
                way = 1 if kz in (0, 2) else 3
                relays["x", kz] = (push(src, relay_x.at[kz], at_y(way)), way)
            else:
                chunk["x", kz, back(ky)] = push(src, xs.at[0, kz, back(ky)], at_y(ky))

    def scatter_g(ky):
        tab, rows = tab_y[ky], tg_y[ky]
        for kz in (2, 1, 3, 0):
            expert = lax.rem(z + kz, N) * N + y
            got = picked(tab, rows, expert, True)
            if kz == 0:
                gs[0, ky, 0] = got
                continue
            send_g[kz - 1, ky] = got
            src = send_g.at[kz - 1, ky]
            if kz == 2:
                way = 1 if ky in (0, 2) else 3
                relays["g", ky] = (push(src, relay_g.at[ky], at_z(way)), way)
            else:
                chunk["g", ky, back(kz)] = push(src, gs.at[0, ky, back(kz)], at_z(kz))

    shared = {}

    def share(name, group, member):
        if member:
            chunk[name, group, member].wait_recv()
        buf = xs if name == "x" else gs
        shared[name, group, member] = push(
            buf.at[0, group, member], buf.at[1, group, member], partner
        )

    def relay(name, group):
        copy, way = relays[name, group]
        copy.wait_recv()
        if name == "x":
            chunk[name, group, 2] = push(relay_x.at[group], xs.at[0, group, 2], at_y(way))
        else:
            chunk[name, group, 2] = push(relay_g.at[group], gs.at[0, group, 2], at_z(way))

    def gate_group(kz):
        for m in range(N):
            shared["x", kz, m].wait_recv()

        @pl.loop(0, HID // TILE)
        def _(n):
            cols = pl.ds(pl.multiple_of(n * TILE, TILE), TILE)
            v = jnp.dot(xs[0, kz].reshape(GROUP, HALF), wg[0, :, cols], preferred_element_type=F32)
            v += jnp.dot(xs[1, kz].reshape(GROUP, HALF), wg[1, :, cols], preferred_element_type=F32)
            gate[kz, :, cols] = v / (1.0 + jnp.exp(-v))

        for h in range(2):

            @pl.loop(0, HALF // TILE)
            def _(n):
                at = pl.multiple_of(n * TILE, TILE)
                block = xs[h, kz, :, :, pl.ds(at, TILE)].reshape(GROUP, TILE)
                xt[pl.ds(pl.multiple_of(h * HALF + at, TILE), TILE), kz * GROUP : (kz + 1) * GROUP] = block.T

    nt = (((1,), (1,)), ((), ()))

    def back_group(ky):
        for m in range(N):
            shared["g", ky, m].wait_recv()

        @pl.loop(0, HID // TILE)
        def _(n):
            cols = pl.ds(pl.multiple_of(n * TILE, TILE), TILE)
            v = lax.dot_general(gs[0, ky].reshape(GROUP, HALF), wd[0, cols, :], nt, preferred_element_type=F32)
            v += lax.dot_general(gs[1, ky].reshape(GROUP, HALF), wd[1, cols, :], nt, preferred_element_type=F32)
            backg[ky, :, cols] = v

    def hidden(kz, ky):
        rows = slice(kz * GROUP + ky * CAP, kz * GROUP + (ky + 1) * CAP)
        hid[rows, :] = (backg[ky, kz * CAP : (kz + 1) * CAP, :] * gate[kz, ky * CAP : (ky + 1) * CAP, :]).astype(BF16)

    own_tok.wait()
    own_tab.wait()
    scatter_x(0)
    own_tg.wait()
    own_tab2.wait()
    scatter_g(0)
    share("x", 0, 0)
    share("g", 0, 0)

    tok_up.wait_recv()
    tok_relay_up = push(tok_z.at[3, pl.ds(0, TOK // 2)], tok_z.at[2, pl.ds(0, TOK // 2)], at_z(1))
    tg_up.wait_recv()
    tg_relay_up = push(tg_y.at[3, pl.ds(0, TOK // 2)], tg_y.at[2, pl.ds(0, TOK // 2)], at_y(1))
    tok_down.wait_recv()
    tok_relay_down = push(
        tok_z.at[1, pl.ds(TOK // 2, TOK // 2)], tok_z.at[2, pl.ds(TOK // 2, TOK // 2)], at_z(3)
    )
    tg_down.wait_recv()
    tg_relay_down = push(
        tg_y.at[1, pl.ds(TOK // 2, TOK // 2)], tg_y.at[2, pl.ds(TOK // 2, TOK // 2)], at_y(3)
    )
    for k in (3, 1):
        tz[back(k)].wait_recv()
        scatter_x(k)
        ty[back(k)].wait_recv()
        scatter_g(k)
        share("x", k, 0)
        share("g", k, 0)
    relay("x", 0)
    relay("g", 0)
    for m in (1, 3):
        share("x", 0, m)
        share("g", 0, m)
    tok_relay_up.wait_recv()
    tok_relay_down.wait_recv()
    tz[2].wait_recv()
    scatter_x(2)
    tg_relay_up.wait_recv()
    tg_relay_down.wait_recv()
    ty[2].wait_recv()
    scatter_g(2)
    share("x", 2, 0)
    share("g", 2, 0)
    for k in (3, 1):
        relay("x", k)
        relay("g", k)
    share("x", 0, 2)
    share("g", 0, 2)
    for load in loads:
        load.wait()
    gate_group(0)
    back_group(0)
    hidden(0, 0)
    for k in (3, 1):
        for m in (1, 3):
            share("x", k, m)
            share("g", k, m)
    relay("x", 2)
    relay("g", 2)
    for k in (3, 1):
        share("x", k, 2)
        share("g", k, 2)
    for k in (3, 1):
        gate_group(k)
        back_group(k)
    for kz in (0, 1, 3):
        for ky in (0, 1, 3):
            if kz or ky:
                hidden(kz, ky)
    for m in (1, 3, 2):
        share("x", 2, m)
        share("g", 2, m)
    gate_group(2)
    back_group(2)
    for k in (0, 1, 3):
        hidden(2, k)
        hidden(k, 2)
    hidden(2, 2)

    part[...] = jnp.zeros_like(part)

    def folded(v):
        s = jnp.sum(v.reshape(v.shape[0] // 8, 8, v.shape[1]), axis=0)
        return sum(s[:, i * 128 : (i + 1) * 128] for i in range(v.shape[1] // 128))

    def gradient(k, store):
        d = lax.rem(x + k, N)
        at = lax.rem(d // 2 + t, 2) * HALF + lax.rem(d, 2) * QUART
        rows = pl.ds(pl.multiple_of(at, QUART), QUART)

        @pl.loop(0, HID // TILE)
        def _(n):
            cols = pl.ds(pl.multiple_of(n * TILE, TILE), TILE)
            v = jnp.dot(xt[rows, :], hid[:, cols], preferred_element_type=F32)
            part[0] += folded(v * v)
            store(cols, v)

    def sending(j):
        def store(cols, v):
            g_send[j, :, cols] = v.astype(BF16)

        return store

    def keeping(cols, v):
        g_own[:, cols] = v

    top, low = pl.ds(0, QUART // 2), pl.ds(QUART // 2, QUART // 2)
    gradient(2, sending(0))
    far_up = push(g_send.at[0, top], g_relay.at[0], at_x(1))
    far_down = push(g_send.at[0, low], g_relay.at[1], at_x(3))
    gradient(1, sending(1))
    near_up = push(g_send.at[1], g_recv.at[3], at_x(1))
    gradient(3, sending(2))
    near_down = push(g_send.at[2], g_recv.at[1], at_x(3))
    gradient(0, keeping)

    slot = [0]

    def gathered(value, pushes):
        first = slot[0]
        slot[0] += 1 + len(pushes)
        tiles[first] = value
        copies = []
        for i, (device, place) in enumerate(pushes):
            copies.append(push(tiles.at[first], tiles.at[first + place], device))
        for copy in copies:
            copy.wait_recv()
        return [tiles[first + i] for i in range(1 + len(pushes))]

    def ring(at):
        return [(at(k), back(k)) for k in (1, 2, 3)]

    def summed(v):
        return (v[0] + v[2]) + (v[1] + v[3])

    def group_sum(value):
        a = gathered(value, [(partner, 1)])
        b = summed(gathered(a[0] + a[1], ring(at_z)))
        return summed(gathered(b, ring(at_y)))

    square = group_sum(part[0])
    far_up.wait_recv()
    far_up2 = push(g_relay.at[0], g_recv.at[2, top], at_x(1))
    far_down.wait_recv()
    far_down2 = push(g_relay.at[1], g_recv.at[2, low], at_x(3))
    squares = gathered(square, ring(at_x))
    scales = []
    for v in squares:
        total = jnp.sum(jnp.sum(v, axis=1, keepdims=True), axis=0, keepdims=True)
        scales.append(jnp.minimum(1.0, math.sqrt(ENTRIES) / jnp.sqrt(total + 1e-06)))

    own_drift.wait()
    for copy in drifts:
        copy.wait_recv()
    near_up.wait_recv()
    near_down.wait_recv()
    far_up2.wait_recv()
    far_down2.wait_recv()

    @pl.loop(0, QUART // 64)
    def _(n):
        rows = pl.ds(pl.multiple_of(n * 64, 64), 64)
        v = scales[0] * g_own[rows, :]
        for k in (1, 2, 3):
            v += scales[k] * g_recv[k, rows, :].astype(F32)
        for k in range(N):
            v += d_recv[k, rows, :].astype(F32)
        v = v * (1.0 / N)
        part[1] += folded(v * v)
        avg_all[0, rows, :] = v.astype(avg_all.dtype)

    up = push(avg_all.at[0], avg_all.at[3], at_x(1))
    down = push(avg_all.at[0], avg_all.at[1], at_x(3))
    outs = [fetch(avg_all.at[0], avg_ref.at[x])]
    b = group_sum(part[1])
    sq_ref[...] = summed(gathered(b, ring(at_x)))
    up.wait_recv()
    up2 = push(avg_all.at[3, top], avg_all.at[2, top], at_x(1))
    outs.append(fetch(avg_all.at[3], avg_ref.at[lax.rem(x + 3, N)]))
    down.wait_recv()
    down2 = push(avg_all.at[1, low], avg_all.at[2, low], at_x(3))
    outs.append(fetch(avg_all.at[1], avg_ref.at[lax.rem(x + 1, N)]))
    up2.wait_recv()
    down2.wait_recv()
    outs.append(fetch(avg_all.at[2], avg_ref.at[lax.rem(x + 2, N)]))
    for copy in started:
        copy.wait_send()
    for copy in outs:
        copy.wait()


def averaged(tokens, token_grads, table, gate_weight, down_weight, drift):
    vm = pltpu.VMEM
    dma = pltpu.SemaphoreType.DMA
    return pl.pallas_call(
        kernel,
        out_shape=(
            jax.ShapeDtypeStruct((N, QUART, HID), AVG),
            jax.ShapeDtypeStruct((8, 128), F32),
        ),
        in_specs=[pl.BlockSpec(memory_space=pl.ANY)] * 6,
        out_specs=(pl.BlockSpec(memory_space=pl.ANY), pl.BlockSpec(memory_space=pltpu.VMEM)),
        scratch_shapes=[
            vm((N, TOK, HALF), BF16),
            vm((N, TOK, HALF), BF16),
            vm((N, CAP, 128), F32),
            vm((N, CAP, 128), F32),
            vm((3, N, CAP, HALF), BF16),
            vm((3, N, CAP, HALF), BF16),
            vm((N, CAP, HALF), BF16),
            vm((N, CAP, HALF), BF16),
            vm((2, N, N, CAP, HALF), BF16),
            vm((2, N, N, CAP, HALF), BF16),
            vm((2, HALF, HID), BF16),
            vm((2, HID, HALF), BF16),
            vm((N, GROUP, HID), F32),
            vm((N, GROUP, HID), F32),
            vm((FEAT, ROWS), BF16),
            vm((ROWS, HID), BF16),
            vm((QUART, HID), F32),
            vm((3, QUART, HID), BF16),
            vm((2, QUART // 2, HID), BF16),
            vm((N, QUART, HID), BF16),
            vm((N, QUART, HID), BF16),
            vm((N, QUART, HID), AVG),
            vm((2, 8, 128), F32),
            vm((32, 8, 128), F32),
            dma((128,)),
            dma((128,)),
            dma((16,)),
        ],
        compiler_params=pltpu.CompilerParams(
            collective_id=0, has_side_effects=True, vmem_limit_bytes=67043328
        ),
        name="averaged",
    )(tokens, token_grads, table, gate_weight, down_weight, drift)


def body(
    tokens,
    token_grads,
    slot_token,
    slot_count,
    slot_prob,
    gate_weight,
    down_weight,
    drift,
    momentum,
):
    index = slot_token[0, 0].T
    live = lax.broadcasted_iota(jnp.int32, index.shape, 0) < slot_count[0, 0][None, :]
    index = jnp.where(live, index.astype(F32), -1.0)
    prob = jnp.where(live, slot_prob[0, 0].T, 0.0)
    table = jnp.concatenate([index, prob, jnp.zeros((CAP, 96), F32)], axis=1)
    average, squares = averaged(
        tokens[0], token_grads[0], table, gate_weight[0, 0], down_weight[0, 0], drift[0, 0]
    )
    average = average.reshape(momentum.shape).astype(F32)
    clip_scale = jnp.minimum(1.0, 0.25 * math.sqrt(ENTRIES) / jnp.sqrt(jnp.sum(squares) + 1e-06))
    clipped = clip_scale * average
    new_moment = 0.9 * momentum + clipped
    return (new_moment, (0.7 * (clipped + 0.9 * new_moment)).astype(BF16))


def solution(mesh):
    return jax.shard_map(
        body,
        mesh=mesh,
        in_specs=(
            P("island", "expert", "tensor"),
            P("island", "expert", "tensor"),
            P("island", "expert", None, None),
            P("island", "expert", None),
            P("island", "expert", None, None),
            P("island", "expert", None, "tensor"),
            P("island", "expert", "tensor", None),
            P("island", "expert", None, "tensor"),
            P("expert", None, "tensor"),
        ),
        out_specs=(P("expert", None, "tensor"), P("expert", None, "tensor")),
        check_vma=False,
    )
```

time: 364 us -> 167 us (0.46)
  waiting for transfers between devices: 151 us -> 0 us
  Pallas kernels: 0 us -> 150 us
  blocking collectives: 109 us -> 0 us
  matrix products: 31.3 us -> 0 us
  other arithmetic: 36.1 us -> 13 us
  local copies, waits for them, and re-layouts: 20.1 us -> 1.65 us
  between operations: 15.5 us -> 1.35 us
    pallas_call x0 -> x1, Pallas kernels: none -> 150 us  [averaged(): pl.pallas_call(kernel, out_shape=(jax.ShapeDtypeStruct((N, QUART, HID), A...]
    psum x1 -> x0, waiting for transfers between devices: 124 us -> none  [body(): average = lax.psum(pseudo, 'island') / islands]
    all_to_all x3 -> x0, blocking collectives: 109 us -> none  [the longest x1 80.6 us: side_by_side(): lax.all_to_all(both, axis, split_axis=split_dim, concat_axis=concat_dim,...]
    dot_general x2 -> x0, matrix products: 31.3 us -> none  [the longest x1 21.8 us: body(): jnp.einsum('erd,erf->edf', inputs, hidden_grad, preferred_element_type=jn...]
    all_gather x1 -> x0, waiting for transfers between devices: 26.8 us -> none  [in_one_piece(): whole, at, done = (lax.all_gather(both, axis, axis=dim, tiled=True), 0, [])]
    gather x2 -> x0, local copies, waits for them, and re-layouts: 17.8 us -> none  [the longest x1 8.88 us: body(): token_grads[0][index_table].astype(jnp.float32)]
    add x1 -> x0, other arithmetic: 7.26 us -> none  [body(): pseudo = drift[0].astype(jnp.float32) + inner_scale * gradient]
    concatenate x2 -> x1, other arithmetic: 5.98 us -> 0.71 us  [body(): table = jnp.concatenate([index, prob, jnp.zeros((CAP, 96), F32)], axis=1)]
  transfers between devices with their start and end apart: 2 -> 0, of which waited for: 2 -> 0; matrix products, arithmetic and copies ran while one was open for 0% -> 0% of each run, Pallas kernels for 0% -> 0%
where the time goes in v1:
time: 167 us; the launch traced here: 166 us
  Pallas kernels  150 us (90%)
  other arithmetic  13 us (8%)
    pallas_call x1, Pallas kernels, averaged(): pl.pallas_call(kernel, out_shape=(jax.ShapeDtypeStruct((N, QUART, HID), A...  150 us
    convert_element_type x1, other arithmetic, body(): return (new_moment, (0.7 * (clipped + 0.9 * new_moment)).astype(BF16))  7.94 us

profile of v1, /device:TPU:1, one launch (start us, length us, event | category | flops | bytes accessed | tf_op | source)
XLA Modules:
  0.0 166.3 jit_solution(17841082961889877868)
XLA Ops:
  0.6 0.1 pad.2.clone
  0.7 0.8 copy.11
  1.5 0.8 copy.12
  2.3 0.7 bitcast_select_fusion.1
  3.0 0.7 maximum_maximum_fusion.tab_ref
  3.7 150.3 %averaged.1 = (bf16[4,512,768]{2,1,0:T(8,128)(2,1)}, f32[8,128]{1,0:T(8,128)}) custom-call(bf16[256,1024]{1,0:T(8,128)(2,1)} %bitcast.27, bf16[256,1024]{1,0:T(8,128)(2,1)} %bitcast.28, f32[96,128]{1,0:T(8,128)} %maximum_maximum_fusion.tab_ref, bf16[2048,768]{1,0:T(8,128)(2,1)} %bitcast.24, bf16[768,2048]{1,0:T(8,128)(2,1)} %bitcast.25, ...), custom_call_target="tpu_custom_call" | custom-call | tf_op jit(solution)/shard_map/averaged/pallas_call | solution.py:401
  153.9 1.3 reduce_sum.9
  155.9 2.4 %convert_multiply_fusion = f32[4,512,768]{2,1,0:T(8,128)S(1)} fusion(bf16[4,512,768]{2,1,0:T(8,128)(2,1)} %get-tuple-element.5, f32[]{:T(128)S(6)} %min_shard_map.3), kind=kLoop, calls=%fused_computation.4 | loop fusion | flops 3145728 | bytes 9437188 | tf_op jit(solution)/shard_map/mul | solution.py:466
  158.3 7.9 %fusion.1 = (bf16[1,2048,768]{2,1,0:T(8,128)(2,1)}, f32[1,2048,768]{2,1,0:T(8,128)}) fusion(f32[1,2048,768]{2,1,0:T(8,128)} %param.17, f32[1,2048,768]{2,1,0:T(8,128)S(1)} %bitcast.23), kind=kLoop, calls=%fused_computation.3 | loop fusion | flops 9437184 | bytes 22020096 | tf_op jit(solution)/shard_map/convert_element_type | solution.py:468
  (1 shorter events, 0.0 us)

commit v2 on v1

v2 whole, which is shorter than its diff:
```python
import functools
import math

import jax
import jax.numpy as jnp
from jax import lax
from jax.experimental import pallas as pl
from jax.experimental.pallas import tpu as pltpu
from jax.sharding import PartitionSpec as P

MESH = pl.DeviceIdType.MESH
BF16 = jnp.bfloat16
F32 = jnp.float32
AVG = jnp.bfloat16
N = 4
CAP = 96
GROUP = N * CAP
ROWS = N * GROUP
TOK = 256
HALF = 1024
FEAT = 2 * HALF
QUART = FEAT // N
HID = 768
TILE = 256
COLS = 256
GCOLS = 256
PIECES = 2
LAST = 256
ENTRIES = 16 * 2048 * 1536


def back(k):
    return (N - k) % N


class Sent:
    def __init__(self, copy):
        self.copy, self.arrived = copy, False

    def wait(self):
        if not self.arrived:
            self.copy.wait()
        self.arrived = True

    def wait_recv(self):
        if not self.arrived:
            self.copy.wait_recv()
        self.arrived = True

    def wait_send(self):
        self.copy.wait_send()


def kernel(
    tok_ref, tg_ref, slot_ref, count_ref, prob_ref, wg_ref, wd_ref, drift_ref,
    avg_ref, scale_ref,
    tok_z, tg_y, tab_z, tab_y, send_x, send_g, relay_x, relay_g, xs, gs, wg, wd,
    gate, backg, xt, hid, g_own, g_far, g_near, g_mine, g_join, g_relay, g_direct, g_recv, d_recv, avg_all,
    part, tiles, slots, counts, probs, table, send_sem, recv_sem, local_sem,
):
    x = lax.axis_index("island")
    ex = lax.axis_index("expert")
    t = lax.axis_index("tensor")
    z, y = ex // N, lax.rem(ex, N)

    def at_x(k):
        return {"island": lax.rem(x + k, N)}

    def at_z(k):
        return {"expert": lax.rem(z + k, N) * N + y}

    def at_y(k):
        return {"expert": z * N + lax.rem(y + k, N)}

    partner = {"tensor": 1 - t}
    started, fetched = [], []

    def push(src, dst, device):
        i = len(started)
        copy = pltpu.make_async_remote_copy(
            src_ref=src, dst_ref=dst, send_sem=send_sem.at[i], recv_sem=recv_sem.at[i],
            device_id=device, device_id_type=MESH,
        )
        copy.start()
        started.append(Sent(copy))
        return started[-1]

    def fetch(src, dst):
        copy = pltpu.make_async_copy(src, dst, local_sem.at[len(fetched)])
        copy.start()
        fetched.append(Sent(copy))
        return fetched[-1]

    own_slots = [fetch(slot_ref, slots), fetch(count_ref, counts), fetch(prob_ref, probs)]
    own_tok = fetch(tok_ref, tok_z.at[0])
    own_tg = fetch(tg_ref, tg_y.at[0])
    mine, theirs = pl.ds(0, HALF), pl.ds(HALF, HALF)
    own_half = pl.ds(pl.multiple_of(t * HALF, HALF), HALF)
    other_half = pl.ds(pl.multiple_of((1 - t) * HALF, HALF), HALF)
    loads = [
        fetch(wg_ref.at[own_half, :], wg.at[mine, :]),
        fetch(wg_ref.at[other_half, :], wg.at[theirs, :]),
        fetch(wd_ref.at[:, own_half], wd.at[:, mine]),
        fetch(wd_ref.at[:, other_half], wd.at[:, theirs]),
    ]

    def quarter(k):
        return pl.ds(pl.multiple_of(lax.rem(x + k, N) * QUART, QUART), QUART)

    own_drift = fetch(drift_ref.at[quarter(0), :], d_recv.at[0])

    barrier = pltpu.get_barrier_semaphore()
    peers = [at(k) for at in (at_x, at_y, at_z) for k in (1, 2, 3)] + [partner]
    for peer in peers:
        pl.semaphore_signal(barrier, inc=1, device_id=peer, device_id_type=MESH)
    pl.semaphore_wait(barrier, len(peers))

    tok_up = push(tok_ref, tok_z.at[3], at_z(1))
    tok_down = push(tok_ref, tok_z.at[1], at_z(3))
    tg_up = push(tg_ref, tg_y.at[3], at_y(1))
    tg_down = push(tg_ref, tg_y.at[1], at_y(3))
    for copy in own_slots:
        copy.wait()
    alive = lax.broadcasted_iota(jnp.int32, (CAP, 16), 0) < counts[...]
    table[...] = jnp.zeros_like(table)
    table[:, 0:16] = jnp.where(alive, slots[...].astype(F32).T, -1.0)
    table[:, 16:32] = jnp.where(alive, probs[...].T, 0.0)
    tz = {k: push(table, tab_z.at[back(k)], at_z(k)) for k in (1, 3, 2)}
    ty = {k: push(table, tab_y.at[back(k)], at_y(k)) for k in (1, 3, 2)}
    drifts = [push(drift_ref.at[quarter(k), :], d_recv.at[back(k)], at_x(k)) for k in (2, 1, 3)]

    lane = lax.broadcasted_iota(jnp.int32, (CAP, 128), 1)
    token_of = lax.broadcasted_iota(jnp.int32, (CAP, TOK), 1).astype(F32)

    def column(tab, at):
        return jnp.sum(jnp.where(lane == at, tab, 0.0), axis=1, keepdims=True)

    def picked(tab, rows, expert, weighted):
        chosen = jnp.where(column(tab, expert) == token_of, 1.0, 0.0).astype(BF16)
        out = jnp.dot(chosen, rows, preferred_element_type=F32)
        if weighted:
            out = out * column(tab, expert + 16)
        return out.astype(BF16)

    chunk = {}
    relays = {}

    def scatter_x(kz):
        tab, rows = (tab_z[kz] if kz else table[...]), tok_z[kz]
        for ky in (2, 1, 3, 0):
            expert = z * N + lax.rem(y + ky, N)
            got = picked(tab, rows, expert, False)
            if ky == 0:
                xs[kz, 0, :, :HALF] = got
                continue
            send_x[ky - 1, kz] = got
            src = send_x.at[ky - 1, kz]
            if ky == 2:
                way = 1 if kz in (0, 2) else 3
                relays["x", kz] = (push(src, relay_x.at[kz], at_y(way)), way)
            else:
                chunk["x", kz, back(ky)] = push(src, xs.at[kz, back(ky), :, mine], at_y(ky))

    def scatter_g(ky):
        tab, rows = (tab_y[ky] if ky else table[...]), tg_y[ky]
        for kz in (2, 1, 3, 0):
            expert = lax.rem(z + kz, N) * N + y
            got = picked(tab, rows, expert, True)
            if kz == 0:
                gs[ky, 0, :, :HALF] = got
                continue
            send_g[kz - 1, ky] = got
            src = send_g.at[kz - 1, ky]
            if kz == 2:
                way = 1 if ky in (0, 2) else 3
                relays["g", ky] = (push(src, relay_g.at[ky], at_z(way)), way)
            else:
                chunk["g", ky, back(kz)] = push(src, gs.at[ky, back(kz), :, mine], at_z(kz))

    shared = {}

    def finish():
        for copy in started:
            copy.wait_recv()
            copy.wait_send()
        for copy in fetched:
            copy.wait()

    def share(name, group, member):
        if member:
            chunk[name, group, member].wait_recv()
        buf = xs if name == "x" else gs
        shared[name, group, member] = push(
            buf.at[group, member, :, mine], buf.at[group, member, :, theirs], partner
        )

    def relay(name, group):
        copy, way = relays[name, group]
        copy.wait_recv()
        if name == "x":
            chunk[name, group, 2] = push(relay_x.at[group], xs.at[group, 2, :, mine], at_y(way))
        else:
            chunk[name, group, 2] = push(relay_g.at[group], gs.at[group, 2, :, mine], at_z(way))

    def gate_group(kz):
        for m in range(N):
            shared["x", kz, m].wait_recv()

        @pl.loop(0, HID // COLS)
        def _(n):
            cols = pl.ds(pl.multiple_of(n * COLS, COLS), COLS)
            v = jnp.dot(xs[kz].reshape(GROUP, FEAT), wg[:, cols], preferred_element_type=F32)
            gate[kz, :, cols] = v / (1.0 + jnp.exp(-v))

        @pl.loop(0, FEAT // TILE)
        def _(n):
            cols = pl.ds(pl.multiple_of(n * TILE, TILE), TILE)
            xt[cols, kz * GROUP : (kz + 1) * GROUP] = xs[kz, :, :, cols].reshape(GROUP, TILE).T

    nt = (((1,), (1,)), ((), ()))

    def back_group(ky):
        for m in range(N):
            shared["g", ky, m].wait_recv()

        @pl.loop(0, HID // COLS)
        def _(n):
            cols = pl.ds(pl.multiple_of(n * COLS, COLS), COLS)
            v = lax.dot_general(
                gs[ky].reshape(GROUP, FEAT), wd[cols, :], nt, preferred_element_type=F32
            )
            backg[ky, :, cols] = v

    def hidden(kz, ky):
        rows = slice(kz * GROUP + ky * CAP, kz * GROUP + (ky + 1) * CAP)
        hid[rows, :] = (backg[ky, kz * CAP : (kz + 1) * CAP, :] * gate[kz, ky * CAP : (ky + 1) * CAP, :]).astype(BF16)

    own_tok.wait()
    scatter_x(0)
    own_tg.wait()
    scatter_g(0)
    share("x", 0, 0)
    share("g", 0, 0)

    tok_up.wait_recv()
    tok_relay_up = push(tok_z.at[3, pl.ds(0, TOK // 2)], tok_z.at[2, pl.ds(0, TOK // 2)], at_z(1))
    tg_up.wait_recv()
    tg_relay_up = push(tg_y.at[3, pl.ds(0, TOK // 2)], tg_y.at[2, pl.ds(0, TOK // 2)], at_y(1))
    tok_down.wait_recv()
    tok_relay_down = push(
        tok_z.at[1, pl.ds(TOK // 2, TOK // 2)], tok_z.at[2, pl.ds(TOK // 2, TOK // 2)], at_z(3)
    )
    tg_down.wait_recv()
    tg_relay_down = push(
        tg_y.at[1, pl.ds(TOK // 2, TOK // 2)], tg_y.at[2, pl.ds(TOK // 2, TOK // 2)], at_y(3)
    )
    for k in (3, 1):
        tz[back(k)].wait_recv()
        scatter_x(k)
        ty[back(k)].wait_recv()
        scatter_g(k)
        share("x", k, 0)
        share("g", k, 0)
    relay("x", 0)
    relay("g", 0)
    for m in (1, 3):
        share("x", 0, m)
        share("g", 0, m)
    for k in (3, 1):
        relay("x", k)
        relay("g", k)
    tok_relay_up.wait_recv()
    tok_relay_down.wait_recv()
    tz[2].wait_recv()
    scatter_x(2)
    tg_relay_up.wait_recv()
    tg_relay_down.wait_recv()
    ty[2].wait_recv()
    scatter_g(2)
    share("x", 0, 2)
    share("g", 0, 2)
    share("x", 2, 0)
    share("g", 2, 0)
    for k in (3, 1):
        for m in (1, 3):
            share("x", k, m)
            share("g", k, m)
    for load in loads:
        load.wait()
    gate_group(0)
    back_group(0)
    hidden(0, 0)
    for k in (3, 1):
        share("x", k, 2)
        share("g", k, 2)
    relay("x", 2)
    relay("g", 2)
    for k in (3, 1):
        gate_group(k)
        back_group(k)
    for kz in (0, 1, 3):
        for ky in (0, 1, 3):
            if kz or ky:
                hidden(kz, ky)
    for m in (1, 3, 2):
        share("x", 2, m)
        share("g", 2, m)
    gate_group(2)
    back_group(2)
    for k in (0, 1, 3):
        hidden(2, k)
        hidden(k, 2)
    hidden(2, 2)

    part[...] = jnp.zeros_like(part)

    def folded(v):
        s = jnp.sum(v.reshape(v.shape[0] // 8, 8, v.shape[1]), axis=0)
        return sum(s[:, i * 128 : (i + 1) * 128] for i in range(v.shape[1] // 128))

    def gradient(k, store):
        d = lax.rem(x + k, N)
        at = lax.rem(d // 2 + t, 2) * HALF + lax.rem(d, 2) * QUART
        rows = pl.ds(pl.multiple_of(at, QUART), QUART)

        @pl.loop(0, HID // GCOLS)
        def _(n):
            cols = pl.ds(pl.multiple_of(n * GCOLS, GCOLS), GCOLS)
            v = jnp.dot(xt[rows, :], hid[:, cols], preferred_element_type=F32)
            part[0] += folded(v * v)
            store(cols, v)

    top, low = pl.ds(0, QUART // 2), pl.ds(QUART // 2, QUART // 2)

    def far(cols, v):
        g_far[:, cols] = v.astype(BF16)

    def up_side(cols, v):
        g_mine[0, :, cols] = v[: QUART // 2]
        g_near[0, :, cols] = v[QUART // 2 :].astype(BF16)

    def down_side(cols, v):
        g_near[1, :, cols] = v[: QUART // 2].astype(BF16)
        g_mine[1, :, cols] = v[QUART // 2 :]

    def keeping(cols, v):
        g_own[:, cols] = v

    gradient(2, far)
    far_up = push(g_far.at[top], g_relay.at[0], at_x(1))
    far_down = push(g_far.at[low], g_relay.at[1], at_x(3))
    gradient(1, up_side)
    near_up = push(g_near.at[0], g_direct.at[1], at_x(1))
    gradient(3, down_side)
    near_down = push(g_near.at[1], g_direct.at[0], at_x(3))
    gradient(0, keeping)

    slot = [0]

    def gathered(value, pushes):
        first = slot[0]
        slot[0] += 1 + len(pushes)
        tiles[first] = value
        copies = []
        for i, (device, place) in enumerate(pushes):
            copies.append(push(tiles.at[first], tiles.at[first + place], device))
        for copy in copies:
            copy.wait_recv()
        return [tiles[first + i] for i in range(1 + len(pushes))]

    def ring(at):
        return [(at(k), back(k)) for k in (1, 2, 3)]

    def summed(v):
        return (v[0] + v[2]) + (v[1] + v[3])

    def group_sum(value):
        a = gathered(value, [(partner, 1)])
        b = summed(gathered(a[0] + a[1], ring(at_z)))
        return summed(gathered(b, ring(at_y)))

    square = group_sum(part[0])
    squares = gathered(square, ring(at_x))
    scales = []
    for v in squares:
        total = jnp.sum(jnp.sum(v, axis=1, keepdims=True), axis=0, keepdims=True)
        scales.append(jnp.minimum(1.0, math.sqrt(ENTRIES) / jnp.sqrt(total + 1e-06)))

    piece = QUART // 2 // PIECES
    joined = []
    for copy in (far_up, far_down):
        copy.wait_recv()
    for p in range(PIECES):
        rows = pl.ds(p * piece, piece)
        for side, way in ((0, 1), (1, 3)):
            from_there = scales[back(way)] * g_relay[side, rows, :].astype(F32)
            g_join[side, rows, :] = (from_there + scales[0] * g_mine[side, rows, :]).astype(BF16)
            joined.append(push(g_join.at[side, rows], g_recv.at[side, rows], at_x(way)))

    own_drift.wait()
    for copy in drifts:
        copy.wait_recv()
    near_up.wait_recv()
    near_down.wait_recv()

    ups, downs = {}, {}
    for p in range(PIECES):
        for side in range(2):
            joined[2 * p + side].wait_recv()
            direct = scales[1] if side == 0 else scales[3]

            @pl.loop(0, piece // 64)
            def _(n):
                at = pl.multiple_of(p * piece + n * 64, 64)
                near = pl.ds(at, 64)
                rows = pl.ds(pl.multiple_of(side * (QUART // 2) + at, 64), 64)
                v = scales[0] * g_own[rows, :]
                v += direct * g_direct[side, near, :].astype(F32)
                v += g_recv[side, near, :].astype(F32)
                for k in range(N):
                    v += d_recv[k, rows, :].astype(F32)
                v = v * (1.0 / N)
                part[1] += folded(v * v)
                avg_all[0, rows, :] = v.astype(avg_all.dtype)

        at = {side: pl.ds(side * (QUART // 2) + p * piece, piece) for side in range(2)}
        for side in (0, 1):
            ups[p, side] = push(avg_all.at[0, at[side]], avg_all.at[3, at[side]], at_x(1))
        for side in (1, 0):
            downs[p, side] = push(avg_all.at[0, at[side]], avg_all.at[1, at[side]], at_x(3))

    fetch(avg_all.at[0], avg_ref.at[quarter(0), :])
    passed = []

    def pass_on(p):
        rows = pl.ds(p * piece, piece)
        ups[p, 0].wait_recv()
        passed.append(push(avg_all.at[3, rows], avg_all.at[2, rows], at_x(1)))
        rows = pl.ds(QUART // 2 + p * piece, piece)
        downs[p, 1].wait_recv()
        passed.append(push(avg_all.at[1, rows], avg_all.at[2, rows], at_x(3)))

    pass_on(0)
    b = group_sum(part[1])
    total = summed(gathered(b, ring(at_x)))
    total = jnp.sum(jnp.sum(total, axis=1, keepdims=True), axis=0, keepdims=True)
    scale = jnp.minimum(1.0, 0.25 * math.sqrt(ENTRIES) / jnp.sqrt(total + 1e-06))
    scale_ref[...] = jnp.broadcast_to(scale, scale_ref.shape)
    for p in range(1, PIECES):
        pass_on(p)
    for p in range(PIECES):
        ups[p, 1].wait_recv()
        downs[p, 0].wait_recv()
    fetch(avg_all.at[3], avg_ref.at[quarter(3), :])
    fetch(avg_all.at[1], avg_ref.at[quarter(1), :])
    for copy in passed:
        copy.wait_recv()
    fetch(avg_all.at[2], avg_ref.at[quarter(2), :])
    finish()


def averaged(tokens, token_grads, slots, counts, probs, gate_weight, down_weight, drift):
    vm = pltpu.VMEM
    dma = pltpu.SemaphoreType.DMA
    return pl.pallas_call(
        kernel,
        out_shape=(
            jax.ShapeDtypeStruct((FEAT, HID), AVG),
            jax.ShapeDtypeStruct((8, 128), F32),
        ),
        in_specs=[pl.BlockSpec(memory_space=pl.ANY)] * 8,
        out_specs=(pl.BlockSpec(memory_space=pl.ANY), pl.BlockSpec(memory_space=pltpu.VMEM)),
        scratch_shapes=[
            vm((N, TOK, HALF), BF16),
            vm((N, TOK, HALF), BF16),
            vm((N, CAP, 128), F32),
            vm((N, CAP, 128), F32),
            vm((3, N, CAP, HALF), BF16),
            vm((3, N, CAP, HALF), BF16),
            vm((N, CAP, HALF), BF16),
            vm((N, CAP, HALF), BF16),
            vm((N, N, CAP, FEAT), BF16),
            vm((N, N, CAP, FEAT), BF16),
            vm((FEAT, HID), BF16),
            vm((HID, FEAT), BF16),
            vm((N, GROUP, HID), F32),
            vm((N, GROUP, HID), F32),
            vm((FEAT, ROWS), BF16),
            vm((ROWS, HID), BF16),
            vm((QUART, HID), F32),
            vm((QUART, HID), BF16),
            vm((2, QUART // 2, HID), BF16),
            vm((2, QUART // 2, HID), F32),
            vm((2, QUART // 2, HID), BF16),
            vm((2, QUART // 2, HID), BF16),
            vm((2, QUART // 2, HID), BF16),
            vm((2, QUART // 2, HID), BF16),
            vm((N, QUART, HID), BF16),
            vm((N, QUART, HID), AVG),
            vm((2, 8, 128), F32),
            vm((32, 8, 128), F32),
            vm((16, CAP), jnp.int32),
            vm((1, 16), jnp.int32),
            vm((16, CAP), F32),
            vm((CAP, 128), F32),
            dma((160,)),
            dma((160,)),
            dma((16,)),
        ],
        compiler_params=pltpu.CompilerParams(
            collective_id=0, has_side_effects=True, vmem_limit_bytes=67043328
        ),
        name="averaged",
    )(tokens, token_grads, slots, counts, probs, gate_weight, down_weight, drift)


def last(scale_ref, avg_ref, old_ref, new_ref, step_ref):
    clipped = scale_ref[0, 0] * avg_ref[...].astype(F32)
    new = 0.9 * old_ref[...] + clipped
    new_ref[...] = new
    step_ref[...] = (0.7 * (clipped + 0.9 * new)).astype(BF16)


def updated(scale, average, momentum):
    block = pl.BlockSpec((LAST, HID), lambda i: (i, 0))
    return pl.pallas_call(
        last,
        grid=(FEAT // LAST,),
        out_shape=(
            jax.ShapeDtypeStruct((FEAT, HID), F32),
            jax.ShapeDtypeStruct((FEAT, HID), BF16),
        ),
        in_specs=[pl.BlockSpec(memory_space=pltpu.SMEM), block, block],
        out_specs=(block, block),
        compiler_params=pltpu.CompilerParams(vmem_limit_bytes=67043328),
        name="updated",
    )(scale, average, momentum)


def body(
    tokens,
    token_grads,
    slot_token,
    slot_count,
    slot_prob,
    gate_weight,
    down_weight,
    drift,
    momentum,
):
    average, scale = averaged(
        tokens[0], token_grads[0], slot_token[0, 0], slot_count[0], slot_prob[0, 0],
        gate_weight[0, 0], down_weight[0, 0], drift[0, 0],
    )
    new_momentum, outer_step = updated(scale, average, momentum[0])
    return (new_momentum[None], outer_step[None])


def solution(mesh):
    return jax.shard_map(
        body,
        mesh=mesh,
        in_specs=(
            P("island", "expert", "tensor"),
            P("island", "expert", "tensor"),
            P("island", "expert", None, None),
            P("island", "expert", None),
            P("island", "expert", None, None),
            P("island", "expert", None, "tensor"),
            P("island", "expert", "tensor", None),
            P("island", "expert", None, "tensor"),
            P("expert", None, "tensor"),
        ),
        out_specs=(P("expert", None, "tensor"), P("expert", None, "tensor")),
        check_vma=False,
    )
```

time: 167 us -> 149 us (0.89)
  other arithmetic: 13 us -> 0 us
  Pallas kernels: 150 us -> 148 us
    convert_element_type x1 -> x0, other arithmetic: 7.94 us -> none  [body(): return (new_moment, (0.7 * (clipped + 0.9 * new_moment)).astype(BF16))]
    pallas_call x1 -> x2, Pallas kernels: 150 us -> 148 us  [the longest x1 138 us: averaged(): pl.pallas_call(kernel, out_shape=(jax.ShapeDtypeStruct((FEAT, HID), AVG),...]
    mul x1 -> x0, other arithmetic: 2.42 us -> none  [body(): clipped = clip_scale * average]
where the time goes in v2:
time: 149 us; the launch traced here: 148 us
  Pallas kernels  148 us (99%)
    pallas_call x1, Pallas kernels, averaged(): pl.pallas_call(kernel, out_shape=(jax.ShapeDtypeStruct((FEAT, HID), AVG),...  138 us
    pallas_call x1, Pallas kernels, updated(): pl.pallas_call(last, grid=(FEAT // LAST,), out_shape=(jax.ShapeDtypeStruc...  9.67 us

profile of v2, /device:TPU:1, one launch (start us, length us, event | category | flops | bytes accessed | tf_op | source)
XLA Modules:
  0.0 148.4 jit_solution(14568741415047101652)
XLA Ops:
  0.6 138.0 %averaged.1 = (bf16[2048,768]{1,0:T(8,128)(2,1)}, f32[8,128]{1,0:T(8,128)}) custom-call(bf16[256,1024]{1,0:T(8,128)(2,1)} %bitcast.15, bf16[256,1024]{1,0:T(8,128)(2,1)} %bitcast.16, s32[16,96]{1,0:T(8,128)} %bitcast.17, s32[1,16]{1,0:T(1,128)} %bitcast.19, f32[16,96]{1,0:T(8,128)} %bitcast.18, bf16[2048,768]{1,0:T(8,128)(2,1)} %bitcast.12, ...), custom_call_target="tpu_custom_call" | custom-call | tf_op jit(solution)/shard_map/averaged/pallas_call | solution.py:465
  138.7 9.7 %updated.1 = (f32[2048,768]{1,0:T(8,128)}, bf16[2048,768]{1,0:T(8,128)(2,1)}) custom-call(f32[8,128]{1,0:T(8,128)} %get-tuple-element.6.scale_ref, bf16[2048,768]{1,0:T(8,128)(2,1)} %get-tuple-element.7.avg_ref, f32[2048,768]{1,0:T(8,128)} %bitcast.11), custom_call_target="tpu_custom_call" | custom-call | tf_op jit(solution)/shard_map/updated/pallas_call | solution.py:526

commit v3 on v2

--- a/solution.py
+++ b/solution.py
@@ -25,6 +25,12 @@
 COLS = 256
 GCOLS = 256
 PIECES = 2
+VMEM_AVERAGED = 55 << 20
+VMEM_UPDATED = 57 << 20
+WAY = (1, 3, 1, 3)
+PLACE = (0, 1, 3, 2)
+SENDS = 56
+COPIES = 107
 LAST = 256
 ENTRIES = 16 * 2048 * 1536
 
@@ -35,7 +41,7 @@
 
 class Sent:
     def __init__(self, copy):
-        self.copy, self.arrived = copy, False
+        self.copy, self.arrived, self.sent = copy, False, False
 
     def wait(self):
         if not self.arrived:
@@ -48,14 +54,16 @@
         self.arrived = True
 
     def wait_send(self):
-        self.copy.wait_send()
+        if not self.sent:
+            self.copy.wait_send()
+        self.sent = True
 
 
 def kernel(
     tok_ref, tg_ref, slot_ref, count_ref, prob_ref, wg_ref, wd_ref, drift_ref,
     avg_ref, scale_ref,
     tok_z, tg_y, tab_z, tab_y, send_x, send_g, relay_x, relay_g, xs, gs, wg, wd,
-    gate, backg, xt, hid, g_own, g_far, g_near, g_mine, g_join, g_relay, g_direct, g_recv, d_recv, avg_all,
+    gate, backg, xt, hid, g_relay, g_direct, g_recv, d_recv, avg_all,
     part, tiles, slots, counts, probs, table, send_sem, recv_sem, local_sem,
 ):
     x = lax.axis_index("island")
@@ -77,8 +85,10 @@
 
     def push(src, dst, device):
         i = len(started)
+        if i >= SENDS:
+            started[i - SENDS].wait_send()
         copy = pltpu.make_async_remote_copy(
-            src_ref=src, dst_ref=dst, send_sem=send_sem.at[i], recv_sem=recv_sem.at[i],
+            src_ref=src, dst_ref=dst, send_sem=send_sem.at[i % SENDS], recv_sem=recv_sem.at[i],
             device_id=device, device_id_type=MESH,
         )
         copy.start()
@@ -121,15 +131,19 @@
     tg_down = push(tg_ref, tg_y.at[1], at_y(3))
     for copy in own_slots:
         copy.wait()
-    alive = lax.broadcasted_iota(jnp.int32, (CAP, 16), 0) < counts[...]
+    across = lax.broadcasted_iota(jnp.int32, (16, 16), 1)
+    diagonal = lax.broadcasted_iota(jnp.int32, (16, 16), 0) == across
+    filled = jnp.sum(jnp.where(diagonal, counts[...], 0), axis=1, keepdims=True)
+    alive = lax.broadcasted_iota(jnp.int32, (16, CAP), 1) < filled
     table[...] = jnp.zeros_like(table)
-    table[:, 0:16] = jnp.where(alive, slots[...].astype(F32).T, -1.0)
-    table[:, 16:32] = jnp.where(alive, probs[...].T, 0.0)
-    tz = {k: push(table, tab_z.at[back(k)], at_z(k)) for k in (1, 3, 2)}
+    table[0:16, 0:CAP] = jnp.where(alive, slots[...].astype(F32), -1.0)
+    table[16:32, 0:CAP] = jnp.where(alive, probs[...], 0.0)
+    names = pl.ds(0, 16)
+    tz = {k: push(table.at[names], tab_z.at[back(k), names], at_z(k)) for k in (1, 3, 2)}
     ty = {k: push(table, tab_y.at[back(k)], at_y(k)) for k in (1, 3, 2)}
     drifts = [push(drift_ref.at[quarter(k), :], d_recv.at[back(k)], at_x(k)) for k in (2, 1, 3)]
 
-    lane = lax.broadcasted_iota(jnp.int32, (CAP, 128), 1)
+    lane = lax.broadcasted_iota(jnp.int32, (CAP, 32), 1)
     token_of = lax.broadcasted_iota(jnp.int32, (CAP, TOK), 1).astype(F32)
 
     def column(tab, at):
@@ -146,7 +160,7 @@
     relays = {}
 
     def scatter_x(kz):
-        tab, rows = (tab_z[kz] if kz else table[...]), tok_z[kz]
+        tab, rows = (tab_z[kz] if kz else table[...]).T[:CAP], tok_z[kz]
         for ky in (2, 1, 3, 0):
             expert = z * N + lax.rem(y + ky, N)
             got = picked(tab, rows, expert, False)
@@ -156,13 +170,12 @@
             send_x[ky - 1, kz] = got
             src = send_x.at[ky - 1, kz]
             if ky == 2:
-                way = 1 if kz in (0, 2) else 3
-                relays["x", kz] = (push(src, relay_x.at[kz], at_y(way)), way)
+                relays["x", kz] = push(src, relay_x.at[kz], at_y(WAY[kz]))
             else:
-                chunk["x", kz, back(ky)] = push(src, xs.at[kz, back(ky), :, mine], at_y(ky))
+                chunk["x", kz, back(ky)] = push(src, xs.at[kz, PLACE[back(ky)], :, mine], at_y(ky))
 
     def scatter_g(ky):
-        tab, rows = (tab_y[ky] if ky else table[...]), tg_y[ky]
+        tab, rows = (tab_y[ky] if ky else table[...]).T[:CAP], tg_y[ky]
         for kz in (2, 1, 3, 0):
             expert = lax.rem(z + kz, N) * N + y
             got = picked(tab, rows, expert, True)
@@ -172,10 +185,9 @@
             send_g[kz - 1, ky] = got
             src = send_g.at[kz - 1, ky]
             if kz == 2:
-                way = 1 if ky in (0, 2) else 3
-                relays["g", ky] = (push(src, relay_g.at[ky], at_z(way)), way)
+                relays["g", ky] = push(src, relay_g.at[ky], at_z(WAY[ky]))
             else:
-                chunk["g", ky, back(kz)] = push(src, gs.at[ky, back(kz), :, mine], at_z(kz))
+                chunk["g", ky, back(kz)] = push(src, gs.at[ky, PLACE[back(kz)], :, mine], at_z(kz))
 
     shared = {}
 
@@ -186,31 +198,32 @@
         for copy in fetched:
             copy.wait()
 
-    def share(name, group, member):
-        if member:
-            chunk[name, group, member].wait_recv()
+    def share(name, group, members):
+        for member in members:
+            if member:
+                chunk[name, group, member].wait_recv()
         buf = xs if name == "x" else gs
-        shared[name, group, member] = push(
-            buf.at[group, member, :, mine], buf.at[group, member, :, theirs], partner
+        places = pl.ds(PLACE[members[0]], len(members))
+        shared.setdefault((name, group), []).append(
+            push(buf.at[group, places, :, mine], buf.at[group, places, :, theirs], partner)
         )
 
     def relay(name, group):
-        copy, way = relays[name, group]
-        copy.wait_recv()
-        if name == "x":
-            chunk[name, group, 2] = push(relay_x.at[group], xs.at[group, 2, :, mine], at_y(way))
-        else:
-            chunk[name, group, 2] = push(relay_g.at[group], gs.at[group, 2, :, mine], at_z(way))
+        held, buf, at = (relay_x, xs, at_y) if name == "x" else (relay_g, gs, at_z)
+        relays[name, group].wait_recv()
+        chunk[name, group, 2] = push(
+            held.at[group], buf.at[group, PLACE[2], :, mine], at(WAY[group])
+        )
 
     def gate_group(kz):
-        for m in range(N):
-            shared["x", kz, m].wait_recv()
+        for copy in shared["x", kz]:
+            copy.wait_recv()
 
         @pl.loop(0, HID // COLS)
         def _(n):
             cols = pl.ds(pl.multiple_of(n * COLS, COLS), COLS)
             v = jnp.dot(xs[kz].reshape(GROUP, FEAT), wg[:, cols], preferred_element_type=F32)
-            gate[kz, :, cols] = v / (1.0 + jnp.exp(-v))
+            gate[pl.ds(kz * GROUP, GROUP), cols] = v / (1.0 + jnp.exp(-v))
 
         @pl.loop(0, FEAT // TILE)
         def _(n):
@@ -220,8 +233,8 @@
     nt = (((1,), (1,)), ((), ()))
 
     def back_group(ky):
-        for m in range(N):
-            shared["g", ky, m].wait_recv()
+        for copy in shared["g", ky]:
+            copy.wait_recv()
 
         @pl.loop(0, HID // COLS)
         def _(n):
@@ -229,19 +242,17 @@
             v = lax.dot_general(
                 gs[ky].reshape(GROUP, FEAT), wd[cols, :], nt, preferred_element_type=F32
             )
-            backg[ky, :, cols] = v
+            backg[pl.ds(ky * GROUP, GROUP), cols] = v
 
     def hidden(kz, ky):
-        rows = slice(kz * GROUP + ky * CAP, kz * GROUP + (ky + 1) * CAP)
-        hid[rows, :] = (backg[ky, kz * CAP : (kz + 1) * CAP, :] * gate[kz, ky * CAP : (ky + 1) * CAP, :]).astype(BF16)
+        rows = pl.ds(kz * GROUP + PLACE[ky] * CAP, CAP)
+        others = pl.ds(ky * GROUP + PLACE[kz] * CAP, CAP)
+        hid[rows, :] = (backg[others, :] * gate[rows, :]).astype(BF16)
 
     own_tok.wait()
     scatter_x(0)
     own_tg.wait()
     scatter_g(0)
-    share("x", 0, 0)
-    share("g", 0, 0)
-
     tok_up.wait_recv()
     tok_relay_up = push(tok_z.at[3, pl.ds(0, TOK // 2)], tok_z.at[2, pl.ds(0, TOK // 2)], at_z(1))
     tg_up.wait_recv()
@@ -259,16 +270,10 @@
         scatter_x(k)
         ty[back(k)].wait_recv()
         scatter_g(k)
-        share("x", k, 0)
-        share("g", k, 0)
     relay("x", 0)
     relay("g", 0)
-    for m in (1, 3):
-        share("x", 0, m)
-        share("g", 0, m)
-    for k in (3, 1):
-        relay("x", k)
-        relay("g", k)
+    share("x", 0, (0, 1, 3))
+    share("g", 0, (0, 1, 3))
     tok_relay_up.wait_recv()
     tok_relay_down.wait_recv()
     tz[2].wait_recv()
@@ -277,34 +282,39 @@
     tg_relay_down.wait_recv()
     ty[2].wait_recv()
     scatter_g(2)
-    share("x", 0, 2)
-    share("g", 0, 2)
-    share("x", 2, 0)
-    share("g", 2, 0)
-    for k in (3, 1):
-        for m in (1, 3):
-            share("x", k, m)
-            share("g", k, m)
+    relay("x", 3)
+    relay("g", 3)
+    share("x", 3, (0, 1, 3))
+    share("g", 3, (0, 1, 3))
+    relay("x", 1)
+    relay("g", 1)
+    share("x", 0, (2,))
+    share("g", 0, (2,))
+    share("x", 1, (0, 1, 3))
+    share("g", 1, (0, 1, 3))
     for load in loads:
         load.wait()
     gate_group(0)
     back_group(0)
     hidden(0, 0)
-    for k in (3, 1):
-        share("x", k, 2)
-        share("g", k, 2)
+    share("x", 3, (2,))
+    share("g", 3, (2,))
     relay("x", 2)
     relay("g", 2)
-    for k in (3, 1):
-        gate_group(k)
-        back_group(k)
+    gate_group(3)
+    back_group(3)
+    share("x", 1, (2,))
+    share("g", 1, (2,))
+    share("x", 2, (0, 1, 3))
+    share("g", 2, (0, 1, 3))
+    gate_group(1)
+    back_group(1)
     for kz in (0, 1, 3):
         for ky in (0, 1, 3):
             if kz or ky:
                 hidden(kz, ky)
-    for m in (1, 3, 2):
-        share("x", 2, m)
-        share("g", 2, m)
+    share("x", 2, (2,))
+    share("g", 2, (2,))
     gate_group(2)
     back_group(2)
     for k in (0, 1, 3):
@@ -312,6 +322,9 @@
         hidden(k, 2)
     hidden(2, 2)
 
+    g_own, g_mine = gate.at[pl.ds(0, QUART)], gate.at[pl.ds(QUART, QUART)]
+    g_far, g_near = wg.at[pl.ds(0, QUART)], wg.at[pl.ds(QUART, QUART)]
+    g_join = wg.at[pl.ds(2 * QUART, QUART)]
     part[...] = jnp.zeros_like(part)
 
     def folded(v):
@@ -336,12 +349,12 @@
         g_far[:, cols] = v.astype(BF16)
 
     def up_side(cols, v):
-        g_mine[0, :, cols] = v[: QUART // 2]
-        g_near[0, :, cols] = v[QUART // 2 :].astype(BF16)
+        g_mine[top, cols] = v[: QUART // 2]
+        g_near[top, cols] = v[QUART // 2 :].astype(BF16)
 
     def down_side(cols, v):
-        g_near[1, :, cols] = v[: QUART // 2].astype(BF16)
-        g_mine[1, :, cols] = v[QUART // 2 :]
+        g_near[low, cols] = v[: QUART // 2].astype(BF16)
+        g_mine[low, cols] = v[QUART // 2 :]
 
     def keeping(cols, v):
         g_own[:, cols] = v
@@ -350,20 +363,22 @@
     far_up = push(g_far.at[top], g_relay.at[0], at_x(1))
     far_down = push(g_far.at[low], g_relay.at[1], at_x(3))
     gradient(1, up_side)
-    near_up = push(g_near.at[0], g_direct.at[1], at_x(1))
+    first, second = pl.ds(0, QUART // 4), pl.ds(QUART // 4, QUART // 4)
+    near = [push(g_near.at[pl.ds(0, QUART // 4)], g_direct.at[1, first], at_x(1))]
     gradient(3, down_side)
-    near_down = push(g_near.at[1], g_direct.at[0], at_x(3))
+    near.append(push(g_near.at[pl.ds(QUART // 2, QUART // 4)], g_direct.at[0, first], at_x(3)))
     gradient(0, keeping)
 
     slot = [0]
 
-    def gathered(value, pushes):
+    def gathered(value, pushes, then=lambda: None):
         first = slot[0]
         slot[0] += 1 + len(pushes)
         tiles[first] = value
         copies = []
         for i, (device, place) in enumerate(pushes):
             copies.append(push(tiles.at[first], tiles.at[first + place], device))
+        then()
         for copy in copies:
             copy.wait_recv()
         return [tiles[first + i] for i in range(1 + len(pushes))]
@@ -379,8 +394,12 @@
         b = summed(gathered(a[0] + a[1], ring(at_z)))
         return summed(gathered(b, ring(at_y)))
 
+    def meanwhile():
+        near.append(push(g_near.at[pl.ds(QUART // 4, QUART // 4)], g_direct.at[1, second], at_x(1)))
+        near.append(push(g_near.at[pl.ds(3 * QUART // 4, QUART // 4)], g_direct.at[0, second], at_x(3)))
+
     square = group_sum(part[0])
-    squares = gathered(square, ring(at_x))
+    squares = gathered(square, ring(at_x), meanwhile)
     scales = []
     for v in squares:
         total = jnp.sum(jnp.sum(v, axis=1, keepdims=True), axis=0, keepdims=True)
@@ -394,14 +413,15 @@
         rows = pl.ds(p * piece, piece)
         for side, way in ((0, 1), (1, 3)):
             from_there = scales[back(way)] * g_relay[side, rows, :].astype(F32)
-            g_join[side, rows, :] = (from_there + scales[0] * g_mine[side, rows, :]).astype(BF16)
-            joined.append(push(g_join.at[side, rows], g_recv.at[side, rows], at_x(way)))
+            both = pl.ds(side * (QUART // 2) + p * piece, piece)
+            g_join[both, :] = (from_there + scales[0] * g_mine[both, :]).astype(BF16)
+            joined.append(push(g_join.at[both], g_recv.at[side, rows], at_x(way)))
 
     own_drift.wait()
     for copy in drifts:
         copy.wait_recv()
-    near_up.wait_recv()
-    near_down.wait_recv()
+    for copy in near:
+        copy.wait_recv()
 
     ups, downs = {}, {}
     for p in range(PIECES):
@@ -473,8 +493,8 @@
         scratch_shapes=[
             vm((N, TOK, HALF), BF16),
             vm((N, TOK, HALF), BF16),
-            vm((N, CAP, 128), F32),
-            vm((N, CAP, 128), F32),
+            vm((N, 32, 128), F32),
+            vm((N, 32, 128), F32),
             vm((3, N, CAP, HALF), BF16),
             vm((3, N, CAP, HALF), BF16),
             vm((N, CAP, HALF), BF16),
@@ -483,15 +503,10 @@
             vm((N, N, CAP, FEAT), BF16),
             vm((FEAT, HID), BF16),
             vm((HID, FEAT), BF16),
-            vm((N, GROUP, HID), F32),
-            vm((N, GROUP, HID), F32),
+            vm((ROWS, HID), F32),
+            vm((ROWS, HID), F32),
             vm((FEAT, ROWS), BF16),
             vm((ROWS, HID), BF16),
-            vm((QUART, HID), F32),
-            vm((QUART, HID), BF16),
-            vm((2, QUART // 2, HID), BF16),
-            vm((2, QUART // 2, HID), F32),
-            vm((2, QUART // 2, HID), BF16),
             vm((2, QUART // 2, HID), BF16),
             vm((2, QUART // 2, HID), BF16),
             vm((2, QUART // 2, HID), BF16),
@@ -502,37 +517,56 @@
             vm((16, CAP), jnp.int32),
             vm((1, 16), jnp.int32),
             vm((16, CAP), F32),
-            vm((CAP, 128), F32),
-            dma((160,)),
-            dma((160,)),
-            dma((16,)),
+            vm((32, 128), F32),
+            dma((SENDS,)),
+            dma((COPIES,)),
+            dma((14,)),
         ],
         compiler_params=pltpu.CompilerParams(
-            collective_id=0, has_side_effects=True, vmem_limit_bytes=67043328
+            collective_id=0, has_side_effects=True, vmem_limit_bytes=VMEM_AVERAGED
         ),
         name="averaged",
     )(tokens, token_grads, slots, counts, probs, gate_weight, down_weight, drift)
 
 
-def last(scale_ref, avg_ref, old_ref, new_ref, step_ref):
-    clipped = scale_ref[0, 0] * avg_ref[...].astype(F32)
-    new = 0.9 * old_ref[...] + clipped
-    new_ref[...] = new
-    step_ref[...] = (0.7 * (clipped + 0.9 * new)).astype(BF16)
+def last(scale_ref, avg_ref, old_ref, new_ref, step_ref, avg, new, step, sems):
+    copies, reads = [], []
+    for i in range(FEAT // LAST):
+        rows = pl.ds(i * LAST, LAST)
+        reads.append(pltpu.make_async_copy(avg_ref.at[rows], avg.at[rows], sems.at[2, i]))
+        reads[-1].start()
+    for i in range(FEAT // LAST):
+        rows = pl.ds(i * LAST, LAST)
+        reads[i].wait()
+        clipped = scale_ref[0, 0] * avg[rows, :].astype(F32)
+        moment = 0.9 * old_ref[rows, :] + clipped
+        new[rows, :] = moment
+        step[rows, :] = (0.7 * (clipped + 0.9 * moment)).astype(BF16)
+        for j, (src, dst) in enumerate(((new, new_ref), (step, step_ref))):
+            copies.append(pltpu.make_async_copy(src.at[rows], dst.at[rows], sems.at[j, i]))
+            copies[-1].start()
+    for copy in copies:
+        copy.wait()
 
 
 def updated(scale, average, momentum):
-    block = pl.BlockSpec((LAST, HID), lambda i: (i, 0))
+    place = pl.BlockSpec(memory_space=pltpu.VMEM)
+    out = pl.BlockSpec(memory_space=pl.ANY)
     return pl.pallas_call(
         last,
-        grid=(FEAT // LAST,),
         out_shape=(
             jax.ShapeDtypeStruct((FEAT, HID), F32),
             jax.ShapeDtypeStruct((FEAT, HID), BF16),
         ),
-        in_specs=[pl.BlockSpec(memory_space=pltpu.SMEM), block, block],
-        out_specs=(block, block),
-        compiler_params=pltpu.CompilerParams(vmem_limit_bytes=67043328),
+        in_specs=[pl.BlockSpec(memory_space=pltpu.SMEM), out, place],
+        out_specs=(out, out),
+        scratch_shapes=[
+            pltpu.VMEM((FEAT, HID), AVG),
+            pltpu.VMEM((FEAT, HID), F32),
+            pltpu.VMEM((FEAT, HID), BF16),
+            pltpu.SemaphoreType.DMA((3, FEAT // LAST)),
+        ],
+        compiler_params=pltpu.CompilerParams(vmem_limit_bytes=VMEM_UPDATED),
         name="updated",
     )(scale, average, momentum)
 

time: 149 us -> 141 us (0.946)
  Pallas kernels: 148 us -> 138 us
    pallas_call x1, Pallas kernels: 138 us -> 131 us  [averaged(): pl.pallas_call(kernel, out_shape=(jax.ShapeDtypeStruct((FEAT, HID), AVG),...]
    pallas_call x1, Pallas kernels: 9.67 us -> 7.74 us  [updated(): pl.pallas_call(last, out_shape=(jax.ShapeDtypeStruct((FEAT, HID), F32), j...]
where the time goes in v3:
time: 141 us; the launch traced here: 139 us
  Pallas kernels  138 us (98%)
    pallas_call x1, Pallas kernels, averaged(): pl.pallas_call(kernel, out_shape=(jax.ShapeDtypeStruct((FEAT, HID), AVG),...  131 us
    pallas_call x1, Pallas kernels, updated(): pl.pallas_call(last, out_shape=(jax.ShapeDtypeStruct((FEAT, HID), F32), j...  7.74 us

profile of v3, /device:TPU:1, one launch (start us, length us, event | category | flops | bytes accessed | tf_op | source)
XLA Modules:
  0.0 139.3 jit_solution(12986006737230632395)
XLA Ops:
  0.6 130.8 %averaged.1 = (bf16[2048,768]{1,0:T(8,128)(2,1)}, f32[8,128]{1,0:T(8,128)}) custom-call(bf16[256,1024]{1,0:T(8,128)(2,1)} %bitcast.15, bf16[256,1024]{1,0:T(8,128)(2,1)} %bitcast.16, s32[16,96]{1,0:T(8,128)} %bitcast.17, s32[1,16]{1,0:T(1,128)} %bitcast.19, f32[16,96]{1,0:T(8,128)} %bitcast.18, bf16[2048,768]{1,0:T(8,128)(2,1)} %bitcast.12, ...), custom_call_target="tpu_custom_call" | custom-call | tf_op jit(solution)/shard_map/averaged/pallas_call | solution.py:485
  131.4 7.7 %updated.1 = (f32[2048,768]{1,0:T(8,128)}, bf16[2048,768]{1,0:T(8,128)(2,1)}) custom-call(f32[8,128]{1,0:T(8,128)} %get-tuple-element.6.scale_ref, bf16[2048,768]{1,0:T(8,128)(2,1)} %get-tuple-element.7.avg_ref, f32[2048,768]{1,0:T(8,128)} %bitcast.11), custom_call_target="tpu_custom_call" | custom-call | tf_op jit(solution)/shard_map/updated/pallas_call | solution.py:555

commit v4 on v3

--- a/solution.py
+++ b/solution.py
@@ -23,14 +23,13 @@
 HID = 768
 TILE = 256
 COLS = 256
-GCOLS = 256
 PIECES = 2
 VMEM_AVERAGED = 55 << 20
 VMEM_UPDATED = 57 << 20
 WAY = (1, 3, 1, 3)
 PLACE = (0, 1, 3, 2)
 SENDS = 56
-COPIES = 107
+COPIES = 111
 LAST = 256
 ENTRIES = 16 * 2048 * 1536
 
@@ -307,14 +306,14 @@
     share("g", 1, (2,))
     share("x", 2, (0, 1, 3))
     share("g", 2, (0, 1, 3))
+    share("x", 2, (2,))
+    share("g", 2, (2,))
     gate_group(1)
     back_group(1)
     for kz in (0, 1, 3):
         for ky in (0, 1, 3):
             if kz or ky:
                 hidden(kz, ky)
-    share("x", 2, (2,))
-    share("g", 2, (2,))
     gate_group(2)
     back_group(2)
     for k in (0, 1, 3):
@@ -331,18 +330,27 @@
         s = jnp.sum(v.reshape(v.shape[0] // 8, 8, v.shape[1]), axis=0)
         return sum(s[:, i * 128 : (i + 1) * 128] for i in range(v.shape[1] // 128))
 
-    def gradient(k, store):
+    def gradient(k, store, then=None):
         d = lax.rem(x + k, N)
         at = lax.rem(d // 2 + t, 2) * HALF + lax.rem(d, 2) * QUART
         rows = pl.ds(pl.multiple_of(at, QUART), QUART)
 
-        @pl.loop(0, HID // GCOLS)
-        def _(n):
-            cols = pl.ds(pl.multiple_of(n * GCOLS, GCOLS), GCOLS)
+        def columns(cols):
             v = jnp.dot(xt[rows, :], hid[:, cols], preferred_element_type=F32)
             part[0] += folded(v * v)
             store(cols, v)
 
+        if then is None:
+
+            @pl.loop(0, HID // TILE)
+            def _(n):
+                columns(pl.ds(pl.multiple_of(n * TILE, TILE), TILE))
+
+        else:
+            for n in range(HID // TILE):
+                columns(pl.ds(n * TILE, TILE))
+                then(pl.ds(n * TILE, TILE))
+
     top, low = pl.ds(0, QUART // 2), pl.ds(QUART // 2, QUART // 2)
 
     def far(cols, v):
@@ -359,9 +367,13 @@
     def keeping(cols, v):
         g_own[:, cols] = v
 
-    gradient(2, far)
-    far_up = push(g_far.at[top], g_relay.at[0], at_x(1))
-    far_down = push(g_far.at[low], g_relay.at[1], at_x(3))
+    far_copies = []
+
+    def send_far(cols):
+        far_copies.append(push(g_far.at[top, cols], g_relay.at[0, :, cols], at_x(1)))
+        far_copies.append(push(g_far.at[low, cols], g_relay.at[1, :, cols], at_x(3)))
+
+    gradient(2, far, send_far)
     gradient(1, up_side)
     first, second = pl.ds(0, QUART // 4), pl.ds(QUART // 4, QUART // 4)
     near = [push(g_near.at[pl.ds(0, QUART // 4)], g_direct.at[1, first], at_x(1))]
@@ -407,7 +419,7 @@
 
     piece = QUART // 2 // PIECES
     joined = []
-    for copy in (far_up, far_down):
+    for copy in far_copies:
         copy.wait_recv()
     for p in range(PIECES):
         rows = pl.ds(p * piece, piece)
@@ -473,9 +485,11 @@
         downs[p, 0].wait_recv()
     fetch(avg_all.at[3], avg_ref.at[quarter(3), :])
     fetch(avg_all.at[1], avg_ref.at[quarter(1), :])
-    for copy in passed:
+    for i, copy in enumerate(passed):
         copy.wait_recv()
-    fetch(avg_all.at[2], avg_ref.at[quarter(2), :])
+        at = i % 2 * (QUART // 2) + i // 2 * piece
+        there = pl.ds(pl.multiple_of(lax.rem(x + 2, N) * QUART + at, piece), piece)
+        fetch(avg_all.at[2, pl.ds(at, piece)], avg_ref.at[there, :])
     finish()
 
 
@@ -520,7 +534,7 @@
             vm((32, 128), F32),
             dma((SENDS,)),
             dma((COPIES,)),
-            dma((14,)),
+            dma((17,)),
         ],
         compiler_params=pltpu.CompilerParams(
             collective_id=0, has_side_effects=True, vmem_limit_bytes=VMEM_AVERAGED

time: 141 us -> 142 us (level)
  Pallas kernels: 138 us -> 140 us
    pallas_call x1, Pallas kernels: 131 us -> 132 us  [averaged(): pl.pallas_call(kernel, out_shape=(jax.ShapeDtypeStruct((FEAT, HID), AVG),...]
where the time goes in v4:
time: 142 us; the launch traced here: 141 us
  Pallas kernels  140 us (99%)
    pallas_call x1, Pallas kernels, averaged(): pl.pallas_call(kernel, out_shape=(jax.ShapeDtypeStruct((FEAT, HID), AVG),...  132 us
    pallas_call x1, Pallas kernels, updated(): pl.pallas_call(last, out_shape=(jax.ShapeDtypeStruct((FEAT, HID), F32), j...  7.74 us

profile of v4, /device:TPU:1, one launch (start us, length us, event | category | flops | bytes accessed | tf_op | source)
XLA Modules:
  0.0 140.8 jit_solution(15433688963519666150)
XLA Ops:
  0.6 132.2 %averaged.1 = (bf16[2048,768]{1,0:T(8,128)(2,1)}, f32[8,128]{1,0:T(8,128)}) custom-call(bf16[256,1024]{1,0:T(8,128)(2,1)} %bitcast.15, bf16[256,1024]{1,0:T(8,128)(2,1)} %bitcast.16, s32[16,96]{1,0:T(8,128)} %bitcast.17, s32[1,16]{1,0:T(1,128)} %bitcast.19, f32[16,96]{1,0:T(8,128)} %bitcast.18, bf16[2048,768]{1,0:T(8,128)(2,1)} %bitcast.12, ...), custom_call_target="tpu_custom_call" | custom-call | tf_op jit(solution)/shard_map/averaged/pallas_call | solution.py:499
  132.9 7.7 %updated.1 = (f32[2048,768]{1,0:T(8,128)}, bf16[2048,768]{1,0:T(8,128)(2,1)}) custom-call(f32[8,128]{1,0:T(8,128)} %get-tuple-element.6.scale_ref, bf16[2048,768]{1,0:T(8,128)(2,1)} %get-tuple-element.7.avg_ref, f32[2048,768]{1,0:T(8,128)} %bitcast.11), custom_call_target="tpu_custom_call" | custom-call | tf_op jit(solution)/shard_map/updated/pallas_call | solution.py:569

commit v5 on v4

--- a/solution.py
+++ b/solution.py
@@ -28,7 +28,7 @@
 VMEM_UPDATED = 57 << 20
 WAY = (1, 3, 1, 3)
 PLACE = (0, 1, 3, 2)
-SENDS = 56
+SENDS = 88
 COPIES = 111
 LAST = 256
 ENTRIES = 16 * 2048 * 1536

time: 142 us -> 142 us (level)
  no operation moved by 1% of the time
where the time goes in v5:
time: 142 us; the launch traced here: 141 us
  Pallas kernels  140 us (99%)
    pallas_call x1, Pallas kernels, averaged(): pl.pallas_call(kernel, out_shape=(jax.ShapeDtypeStruct((FEAT, HID), AVG),...  132 us
    pallas_call x1, Pallas kernels, updated(): pl.pallas_call(last, out_shape=(jax.ShapeDtypeStruct((FEAT, HID), F32), j...  7.74 us

profile of v5, /device:TPU:1, one launch (start us, length us, event | category | flops | bytes accessed | tf_op | source)
XLA Modules:
  0.0 140.9 jit_solution(9779300571380071586)
XLA Ops:
  0.6 132.4 %averaged.1 = (bf16[2048,768]{1,0:T(8,128)(2,1)}, f32[8,128]{1,0:T(8,128)}) custom-call(bf16[256,1024]{1,0:T(8,128)(2,1)} %bitcast.15, bf16[256,1024]{1,0:T(8,128)(2,1)} %bitcast.16, s32[16,96]{1,0:T(8,128)} %bitcast.17, s32[1,16]{1,0:T(1,128)} %bitcast.19, f32[16,96]{1,0:T(8,128)} %bitcast.18, bf16[2048,768]{1,0:T(8,128)(2,1)} %bitcast.12, ...), custom_call_target="tpu_custom_call" | custom-call | tf_op jit(solution)/shard_map/averaged/pallas_call | solution.py:499
  133.0 7.7 %updated.1 = (f32[2048,768]{1,0:T(8,128)}, bf16[2048,768]{1,0:T(8,128)(2,1)}) custom-call(f32[8,128]{1,0:T(8,128)} %get-tuple-element.6.scale_ref, bf16[2048,768]{1,0:T(8,128)(2,1)} %get-tuple-element.7.avg_ref, f32[2048,768]{1,0:T(8,128)} %bitcast.11), custom_call_target="tpu_custom_call" | custom-call | tf_op jit(solution)/shard_map/updated/pallas_call | solution.py:569
